TPU v7x, 32 devices: a whole 2x2x4 slice. The times are simulated.
32 devices in a mesh: grp: 2 (over y), sta: 4 (over z), band: 4 (over x, core), src: 1.
Axes of the slice: x: 2, y: 2, z: 4, core: 2. Of those that a mesh axis runs over, the one named last changes fastest.
Arguments:
- spectra: float32 [1, 192, 1024], P('src', ('grp', 'sta', 'band')), parts along dimension 1, may hold values from -6 to 6
- station_place: int32 [192], P('grp'), parts along dimension 0, may hold values from 0 to 95, each once
- tiles: int32 [32, 2], P(('grp', 'sta', 'band')), parts along dimension 0, may hold values from 0 to 1
- observed: float32 [32, 48, 48, 256], P(('grp', 'sta', 'band')), parts along dimension 0, may hold values from -8 to 8
Outputs:
- adjoint: float32 [1, 192, 1024], P('src', ('grp', 'sta', 'band')), parts along dimension 1
There are 2 independent parts, one for each index of `grp`. A program takes and returns all parts, laid end to end along the dimension named above; each array names one. Nothing has to cross between parts.
Inputs may be any that keep to these rules, and one draw needn't show every extreme that they name: station_place is a permutation; block of station s is station_place[s] // 48.
All inputs are finite; a program needn't handle non-finite values.
Results may differ from a plain program's by a relative error of at most 0.00013.
Values sent between devices are 32-bit elements; how exact they have to be, the bound alone decides.
A program may use at most 64 MiB of HBM per device.

v0:
```python
import math

import jax
import jax.numpy as jnp
from jax import lax
from jax.sharding import PartitionSpec as P

cubic_weight = 0.1


def dft_table(freqs, lags):
    fvals = jnp.arange(freqs, dtype=jnp.float32)
    tvals = jnp.arange(lags, dtype=jnp.float32) - lags // 2
    phase = math.pi / freqs * fvals[:, None] * tvals[None, :]
    return jnp.concatenate([jnp.cos(phase), -jnp.sin(phase)], 0) * (1.0 / math.sqrt(freqs))


def cross_spectrum(left, right):
    half = left.shape[-1] // 2
    lre = left[:, :, None, :half]
    lim = left[:, :, None, half:]
    rre = right[:, None, :, :half]
    rim = right[:, None, :, half:]
    real = jnp.sum(lre * rre + lim * rim, axis=0)
    imag = jnp.sum(lim * rre - lre * rim, axis=0)
    return jnp.concatenate([real, imag], -1)


def adjoint_terms(spectral, left, right):
    half = left.shape[-1] // 2
    are = spectral[:, :, :half]
    aim = spectral[:, :, half:]
    highest = lax.Precision.HIGHEST
    lre, lim = (left[:, :, :half], left[:, :, half:])
    rre, rim = (right[:, :, :half], right[:, :, half:])
    row_re = jnp.einsum("pqf,sqf->spf", are, rre, precision=highest) - jnp.einsum(
        "pqf,sqf->spf", aim, rim, precision=highest
    )
    row_im = jnp.einsum("pqf,sqf->spf", are, rim, precision=highest) + jnp.einsum(
        "pqf,sqf->spf", aim, rre, precision=highest
    )
    col_re = jnp.einsum("pqf,spf->sqf", are, lre, precision=highest) + jnp.einsum(
        "pqf,spf->sqf", aim, lim, precision=highest
    )
    col_im = jnp.einsum("pqf,spf->sqf", are, lim, precision=highest) - jnp.einsum(
        "pqf,spf->sqf", aim, lre, precision=highest
    )
    rows = jnp.concatenate([row_re, row_im], -1)
    cols = jnp.concatenate([col_re, col_im], -1)
    return jnp.concatenate([rows, cols], 1)


def local(spectra, station_place, tiles, observed):
    tile = observed.shape[1]
    lags = observed.shape[3]
    width = spectra.shape[2]
    slots = tiles.shape[0]
    count = station_place.shape[0]
    table = dft_table(width // 2, lags)
    highest = lax.Precision.HIGHEST
    whole = lax.all_gather(spectra[0], ("sta", "band"), axis=0, tiled=True)
    holder = (
        jnp.zeros((count,), jnp.int32).at[station_place].set(jnp.arange(count, dtype=jnp.int32))
    )
    offsets = jnp.arange(tile, dtype=jnp.int32)
    wanted = (tiles[:, :, None] * tile + offsets[None, None, :]).reshape(-1)
    fetched = jnp.take(whole, holder[wanted], axis=0).reshape(slots, 2, tile, width)
    slot = 0
    cross = cross_spectrum(fetched[slot, 0][None], fetched[slot, 1][None]).reshape(
        tile * tile, width
    )
    partial_lags = [jnp.dot(cross, table, precision=highest, preferred_element_type=jnp.float32)]
    lagged = lax.psum(jnp.stack(partial_lags, 0), "src")
    slot = 0
    misfit = lagged[slot] - observed[slot].reshape(tile * tile, lags)
    weighted = misfit + cubic_weight * misfit * misfit * misfit
    spectral = jnp.dot(weighted, table.T, precision=highest, preferred_element_type=jnp.float32)
    terms = adjoint_terms(
        spectral.reshape(tile, tile, width), fetched[slot, 0][None], fetched[slot, 1][None]
    )
    pieces = terms[0]
    select = (station_place[:, None] == wanted[None, :]).astype(jnp.float32)
    mine = lax.psum_scatter(
        jnp.dot(select, pieces, precision=highest, preferred_element_type=jnp.float32),
        ("sta", "band"),
        scatter_dimension=0,
        tiled=True,
    )
    return (mine * (1.0 / tile))[None]


def solution(mesh):
    placed = (
        P("src", ("grp", "sta", "band"), None),
        P("grp"),
        P(("grp", "sta", "band"), None),
        P(("grp", "sta", "band"), None, None, None),
    )
    return jax.shard_map(
        local,
        mesh=mesh,
        in_specs=placed,
        out_specs=P("src", ("grp", "sta", "band"), None),
        check_vma=False,
    )
```

profile of v0, /device:TPU:0, one launch (start us, length us, event | category | flops | bytes accessed | tf_op | source)
XLA Modules:
  0.0 95.4 jit_solution(15691845118605126946)
XLA Ops:
  0.0 0.7 multiply_bitcast_fusion
  0.7 0.1 add.110
  0.7 0.1 add.116
  0.8 0.1 add.118
  0.9 0.7 compare_select_fusion.3
  1.6 0.9 scatter_custom_fusion
  2.5 1.2 %gather_fusion = s32[96]{0:T(128)S(1)} fusion(s32[96]{0:T(128)S(1)} %scatter_custom_fusion, s32[1024]{0:T(1024)S(1)} %pad_clamp_fusion.1), kind=kCustom, calls=%fused_computation | custom fusion | bytes 1152 | tf_op jit(solution)/shard_map/gather | solution.py:67
  3.7 0.1 gather.14
  3.8 0.1 add.111
  3.9 24.4 %all-gather = f32[1,96,1024]{2,0,1:T(1,128)S(1)} all-gather(f32[1,6,1024]{2,0,1:T(1,128)} %param.4), channel_id=2, replica_groups=mesh['grp'=2,'sta'=4,'band'=4,'src'=1] {'sta','band'}, dimensions={1}, use_global_device_ids=true | all-gather | bytes 417792 | tf_op jit(solution)/shard_map/all_gather | solution.py:61
  28.3 0.1 copy.64
  28.4 0.7 gather_fusion.1
  29.1 0.1 broadcast_select_fusion
  29.3 0.1 add.113
  29.3 0.1 slice_bitcast_fusion.6
  29.4 1.9 %multiply_cosine_fusion = (f32[512,256]{1,0:T(8,128)S(1)}, f32[512,256]{1,0:T(8,128)S(1)}) fusion(f32[256]{0:T(256)S(1)} %iota_add_fusion, f32[512]{0:T(512)S(1)} %iota_multiply_fusion), kind=kLoop, calls=%fused_computation.24 | loop fusion | flops 262144 | bytes 1051648 | tf_op jit(solution)/shard_map/cos | solution.py:15
  31.4 1.5 %multiply_add_fusion = (f32[48,48,512]{2,1,0:T(8,128)S(1)}, f32[48,48,512]{2,1,0:T(8,128)S(1)}) fusion(f32[48,512]{1,0:T(8,128)S(1)} %get-tuple-element.32, f32[48,512]{1,0:T(8,128)S(1)} %get-tuple-element.27, f32[48,512]{1,0:T(8,128)S(1)} %get-tuple-element.31, f32[48,512]{1,0:T(8,128)S(1)} %get-tuple-element.28), kind=kLoop, calls=%fused_computation.16 | loop fusion | flops 7077888 | bytes 9830400 | tf_op jit(solution)/shard_map/add | solution.py:24
  32.9 8.3 %fusion.1 = f32[2304,256]{1,0:T(8,128)S(1)} fusion(f32[2304,512]{1,0:T(8,128)S(1)} %bitcast.101, f32[2304,512]{1,0:T(8,128)S(1)} %bitcast.100, f32[512,256]{1,0:T(8,128)S(1)} %get-tuple-element.30, f32[512,256]{1,0:T(8,128)S(1)} %get-tuple-element.29), kind=kOutput, calls=%fused_computation.3 | convolution fusion | flops 7250640896 | bytes 12845056 | tf_op jit(solution)/shard_map/dot_general | solution.py:72
  41.2 8.1 %fusion.5 = f32[48,48,1024]{2,1,0:T(8,128)S(1)} fusion(f32[48,48,256]{2,1,0:T(8,128)S(1)} %bitcast.102, f32[1,48,48,256]{3,2,1,0:T(8,128)S(1)} %copy-done, f32[512,256]{1,0:T(8,128)S(1)} %get-tuple-element.30, f32[512,256]{1,0:T(8,128)S(1)} %get-tuple-element.29), kind=kOutput, calls=%fused_computation.18 | convolution fusion | flops 7251230720 | bytes 15204352 | tf_op jit(solution)/shard_map/dot_general | solution.py:77
  49.2 3.1 %multiply_reduce_fusion.6 = (f32[512,48]{0,1:T(8,128)S(1)}, f32[512,48]{0,1:T(8,128)S(1)}, f32[512,48]{0,1:T(8,128)S(1)}, f32[512,48]{0,1:T(8,128)S(1)}) fusion(f32[48,48,1024]{2,1,0:T(8,128)S(1)} %fusion.5, f32[512,48]{0,1:T(8,128)S(1)} %get-tuple-element.33, f32[512,48]{0,1:T(8,128)S(1)} %get-tuple-element.34), kind=kLoop, calls=%fused_computation.13 | loop fusion | flops 9338880 | bytes 10027008 | tf_op jit(solution)/shard_map/pqf,sqf->spf/dot_general | solution.py:36
  52.4 0.0 copy-start.2
  52.5 1.7 %multiply_reduce_fusion.2 = (f32[512,48]{0,1:T(8,128)S(1)}, f32[512,48]{0,1:T(8,128)S(1)}, f32[512,48]{0,1:T(8,128)S(1)}, f32[512,48]{0,1:T(8,128)S(1)}) fusion(f32[48,48,1024]{2,1,0:T(8,128)S(1)} %fusion.5, f32[512,48]{0,1:T(8,128)S(1)} %get-tuple-element.26, f32[512,48]{0,1:T(8,128)S(1)} %get-tuple-element.25), kind=kLoop, calls=%fused_computation.9 | loop fusion | flops 9338880 | bytes 10027008 | tf_op jit(solution)/shard_map/pqf,spf->sqf/dot_general | solution.py:42
  54.2 0.4 fusion.11
  54.6 32.8 %fusion = f32[8,1024]{1,0:T(8,128)S(1)} fusion(f32[96,1024]{1,0:T(8,128)S(1)} %fusion.11), kind=kCustom, calls=%all-reduce-scatter | all-reduce-scatter fusion | flops 131073 | bytes 426496
  87.4 1.4 %collective-permute-start = (f32[8,1024]{1,0:T(8,128)S(1)}, f32[8,1024]{1,0:T(8,128)S(1)}, u32[]{:S(2)}, u32[]{:S(2)}) collective-permute-start(f32[8,1024]{1,0:T(8,128)S(1)} %fusion), channel_id=1, source_target_pairs={{0,1},{1,2},{2,3},{3,4},{4,5},{5,6},{6,7},{7,8},{8,9},{9,10},{10,1... | collective-permute-start | bytes 98312
  88.8 1.3 %collective-permute-start.1 = (f32[8,1024]{1,0:T(8,128)S(1)}, f32[8,1024]{1,0:T(8,128)S(1)}, u32[]{:S(2)}, u32[]{:S(2)}) collective-permute-start(f32[8,1024]{1,0:T(8,128)S(1)} %fusion), channel_id=1, source_target_pairs={{0,2},{1,3},{2,4},{3,5},{4,6},{5,7},{6,8},{7,9},{8,10},{9,11},{10,... | collective-permute-start | bytes 98312
  90.1 1.3 %collective-permute-start.2 = (f32[8,1024]{1,0:T(8,128)S(1)}, f32[8,1024]{1,0:T(8,128)S(1)}, u32[]{:S(2)}, u32[]{:S(2)}) collective-permute-start(f32[8,1024]{1,0:T(8,128)S(1)} %fusion), channel_id=1, source_target_pairs={{0,3},{1,4},{2,5},{3,6},{4,7},{5,8},{6,9},{7,10},{8,11},{9,12},{10... | collective-permute-start | bytes 98312
  91.4 1.3 %collective-permute-start.3 = (f32[6,1024]{1,0:T(8,128)S(1)}, f32[6,1024]{1,0:T(8,128)S(1)}, u32[]{:S(2)}, u32[]{:S(2)}) collective-permute-start(f32[6,1024]{1,0:T(8,128)S(1)} %slice.50), channel_id=1, source_target_pairs={{0,4},{1,5},{2,6},{3,7},{4,8},{5,9},{6,10},{7,11},{8,12},{9,13},{1... | collective-permute-start | bytes 73736
  92.7 0.6 dynamic-slice.4
  94.0 0.3 collective-permute-done.3
  94.3 0.4 concatenate.21
  94.8 0.6 copy.9
  (26 shorter events, 0.2 us)
Async XLA Ops:
  32.8 8.3 %copy-start = (f32[1,48,48,256]{3,2,1,0:T(8,128)S(1)}, f32[1,48,48,256]{3,2,1,0:T(8,128)}, u32[]{:S(2)}) copy-start(f32[1,48,48,256]{3,2,1,0:T(8,128)} %param.7) | copy-start | bytes 7077892
  52.4 1.8 %copy-start.1 = (s32[96]{0:T(128)S(1)}, s32[96]{0:T(128)}, u32[]{:S(2)}) copy-start(s32[96]{0:T(128)} %param.5) | copy-start | bytes 1156
  52.4 40.3 %copy-start.2 = (u32[32]{0:T(128)S(1)}, u32[32]{0:T(128)}, u32[]{:S(2)}) copy-start(u32[32]{0:T(128)} %constant.45) | copy-start | bytes 388
  87.4 6.9 %collective-permute-start = (f32[8,1024]{1,0:T(8,128)S(1)}, f32[8,1024]{1,0:T(8,128)S(1)}, u32[]{:S(2)}, u32[]{:S(2)}) collective-permute-start(f32[8,1024]{1,0:T(8,128)S(1)} %fusion), channel_id=1, source_target_pairs={{0,1},{1,2},{2,3},{3,4},{4,5},{5,6},{6,7},{7,8},{8,9},{9,10},{10,1... | collective-permute-start | bytes 98312
  88.8 5.5 %collective-permute-start.1 = (f32[8,1024]{1,0:T(8,128)S(1)}, f32[8,1024]{1,0:T(8,128)S(1)}, u32[]{:S(2)}, u32[]{:S(2)}) collective-permute-start(f32[8,1024]{1,0:T(8,128)S(1)} %fusion), channel_id=1, source_target_pairs={{0,2},{1,3},{2,4},{3,5},{4,6},{5,7},{6,8},{7,9},{8,10},{9,11},{10,... | collective-permute-start | bytes 98312
  90.1 4.2 %collective-permute-start.2 = (f32[8,1024]{1,0:T(8,128)S(1)}, f32[8,1024]{1,0:T(8,128)S(1)}, u32[]{:S(2)}, u32[]{:S(2)}) collective-permute-start(f32[8,1024]{1,0:T(8,128)S(1)} %fusion), channel_id=1, source_target_pairs={{0,3},{1,4},{2,5},{3,6},{4,7},{5,8},{6,9},{7,10},{8,11},{9,12},{10... | collective-permute-start | bytes 98312
  91.4 2.9 %collective-permute-start.3 = (f32[6,1024]{1,0:T(8,128)S(1)}, f32[6,1024]{1,0:T(8,128)S(1)}, u32[]{:S(2)}, u32[]{:S(2)}) collective-permute-start(f32[6,1024]{1,0:T(8,128)S(1)} %slice.50), channel_id=1, source_target_pairs={{0,4},{1,5},{2,6},{3,7},{4,8},{5,9},{6,10},{7,11},{8,12},{9,13},{1... | collective-permute-start | bytes 73736
where the time goes:
time: 97 us; the launch traced here: 95.4 us
  blocking collectives  57.2 us (59%)
  matrix products  16.7 us (17%)
  other arithmetic  9.75 us (10%)
  starting transfers between devices  5.32 us (5%)
  local copies, waits for them, and re-layouts  5.2 us (5%)
    unnamed x1, blocking collectives  32.8 us
    all_gather x1, blocking collectives, local(): whole = lax.all_gather(spectra[0], ('sta', 'band'), axis=0, tiled=True)  24.4 us
    dot_general x1, matrix products, local(): jnp.dot(cross, table, precision=highest, preferred_element_type=jnp.float32)  8.3 us
    dot_general x1, matrix products, local(): jnp.dot(weighted, table.T, precision=highest, preferred_element_type=jnp....  8.07 us
    unnamed x4, starting transfers between devices  5.32 us
    dot_general x1, other arithmetic, adjoint_terms(): jnp.einsum('pqf,sqf->spf', aim, rim, precision=highest)  3.14 us
  transfers between devices with their start and end apart: 4, of which 1 were waited for; matrix products, arithmetic and copies ran while one was open for 1% of the time, Pallas kernels for 0%

commit v1 on v0

--- a/solution.py
+++ b/solution.py
@@ -1,11 +1,17 @@
+import functools
 import math
 
 import jax
 import jax.numpy as jnp
+import numpy as np
 from jax import lax
+from jax.experimental import pallas as pl
+from jax.experimental.pallas import tpu as pltpu
 from jax.sharding import PartitionSpec as P
 
 cubic_weight = 0.1
+LANES = 128
+MESH = pl.DeviceIdType.MESH
 
 
 def dft_table(freqs, lags):
@@ -88,6 +94,277 @@
     )
     return (mine * (1.0 / tile))[None]
 
+def tables(freqs, lags, lanes):
+    fvals = np.arange(freqs, dtype=np.float64)
+    tvals = np.arange(lags, dtype=np.float64) - lags // 2
+    phase = math.pi / freqs * fvals[:, None] * tvals[None, :]
+    scale = 1.0 / math.sqrt(freqs)
+    chunks = freqs // lanes
+    table = np.stack([np.cos(phase), -np.sin(phase)], 0) * scale
+    table = table.reshape(2, chunks, lanes, lags).transpose(1, 0, 2, 3)
+    table = table.reshape(chunks, 2 * lanes, lags).astype(np.float32)
+    high = table.astype(jnp.bfloat16)
+    low = (table - high.astype(np.float32)).astype(jnp.bfloat16)
+    down = np.stack([high, low], 0)
+    return down, np.ascontiguousarray(down.transpose(0, 1, 3, 2))
+
+
+def split(value):
+    high = value.astype(jnp.bfloat16)
+    return high, (value - high.astype(jnp.float32)).astype(jnp.bfloat16)
+
+
+def mm(a, b):
+    return jnp.dot(a, b, preferred_element_type=jnp.float32)
+
+
+def fused(mesh_sizes, dims, pair_ref, place_ref, spectra_hbm, observed_hbm, down_hbm, up_hbm, out_ref,
+          gath, seen, down, up, lag, whigh, wlow, fetched, acc, sendbuf, halfbuf, sumbuf, recvbuf,
+          load_sem, table_sem, g1send, g1recv, g2send, g2recv, s1send, s1recv, s2send, s2recv):
+    n_sta, n_band = mesh_sizes
+    tile, rows, pad, lanes, chunks, block = dims
+    n = n_sta * n_band
+    pairs = n // 2
+    me = lax.axis_index("sta") * n_band + lax.axis_index("band")
+    mine, core = me // 2, lax.rem(me, 2)
+    real_rows = pl.ds(0, rows)
+
+    def device(pair, side):
+        peer = pair * 2 + side
+        return {"sta": peer // n_band, "band": lax.rem(peer, n_band)}
+
+    def other(k):
+        return lax.rem(mine + k, pairs)
+
+    own = [
+        pltpu.make_async_copy(
+            spectra_hbm.at[r, pl.ds(h * chunks, chunks), :],
+            gath.at[pl.ds(0, chunks), core, mine, r, pl.ds(h * lanes, lanes)],
+            load_sem.at[r, h],
+        )
+        for r in range(rows) for h in range(2)
+    ]
+    for load in own:
+        load.start()
+    loads = [
+        pltpu.make_async_copy(down_hbm, down, table_sem.at[0]),
+        pltpu.make_async_copy(observed_hbm, seen, table_sem.at[1]),
+        pltpu.make_async_copy(up_hbm, up, table_sem.at[2]),
+    ]
+    for load in loads:
+        load.start()
+
+    barrier = pltpu.get_barrier_semaphore()
+
+    @pl.loop(1, pairs)
+    def _(k):
+        pl.semaphore_signal(barrier, inc=1, device_id=device(other(k), core), device_id_type=MESH)
+
+    pl.semaphore_signal(barrier, inc=1, device_id=device(mine, 1 - core), device_id_type=MESH)
+    pl.semaphore_wait(barrier, pairs)
+
+    def remote(src, dst, send, recv, pair, side):
+        return pltpu.make_async_remote_copy(
+            src_ref=src, dst_ref=dst, send_sem=send, recv_sem=recv,
+            device_id=device(pair, side), device_id_type=MESH,
+        )
+
+    def spread(c, k, holder):
+        part = gath.at[c, core, holder, real_rows, :]
+        return remote(part, part, g1send.at[c, k], g1recv.at[c, k], other(k), core)
+
+    def forward(c, side):
+        part = gath.at[c, side, :, real_rows, :]
+        return remote(part, part, g2send.at[c], g2recv.at[c], mine, 1 - core)
+
+    def relay(c):
+        @pl.loop(1, pairs)
+        def _(k):
+            spread(c, k, lax.rem(mine + pairs - k, pairs)).wait_recv()
+
+        forward(c, core).start()
+
+    for load in own:
+        load.wait()
+    for c in range(chunks):
+        @pl.loop(1, pairs)
+        def _(k):
+            spread(c, k, mine).start()
+
+    count = n * rows
+    f32 = jnp.float32
+    s_idx = lax.broadcasted_iota(jnp.int32, (count, n * pad), 0)
+    g_idx = lax.broadcasted_iota(jnp.int32, (count, n * pad), 1)
+    holder = s_idx // rows
+    s_row = (holder % 2 * pairs + holder // 2) * pad + s_idx % rows
+    expand = (s_row == g_idx).astype(f32)
+    places = jnp.broadcast_to(place_ref[...].astype(f32) + 1.0, (8, count))
+    places = lax.dot(places, expand, precision=lax.Precision.HIGHEST, preferred_element_type=f32)
+    places = jnp.broadcast_to(places[0:1, :], (2 * tile, n * pad))
+    j_idx = lax.broadcasted_iota(jnp.int32, (2 * tile, n * pad), 0)
+    wanted = jnp.where(j_idx < tile, pair_ref[0, 0] * tile + j_idx, pair_ref[0, 1] * tile + j_idx - tile)
+    select32 = (jnp.abs(places - 1.0 - wanted.astype(f32)) < 0.5).astype(f32)
+    select = select32.astype(jnp.bfloat16)
+    back = jnp.transpose(select32).astype(jnp.bfloat16)
+    valid = lax.broadcasted_iota(jnp.int32, (n * pad, 2 * lanes), 0) % pad < rows
+
+    relay(0)
+    loads[0].wait()
+    steps = tile // block
+    span = block * tile
+    for c in range(chunks):
+        if c + 1 < chunks:
+            relay(c + 1)
+        forward(c, 1 - core).wait_recv()
+        whole = jnp.where(valid, gath[c].reshape(n * pad, 2 * lanes), 0.0)
+        high, rest = split(whole)
+        low = (whole - high.astype(f32) - rest.astype(f32)).astype(jnp.bfloat16)
+        fetched[c] = mm(select, high) + mm(select, rest) + mm(select, low)
+
+        @pl.loop(0, steps)
+        def _(b):
+            p0 = pl.multiple_of(b * block, block)
+            at = pl.ds(pl.multiple_of(b * span, span), span)
+            left = fetched[c, pl.ds(p0, block), :]
+            lre, lim = left[:, None, :lanes], left[:, None, lanes:]
+            right = fetched[c, pl.ds(tile, tile), :]
+            rre, rim = right[None, :, :lanes], right[None, :, lanes:]
+            real = (lre * rre + lim * rim).reshape(span, lanes)
+            imag = (lim * rre - lre * rim).reshape(span, lanes)
+            high, low = split(jnp.concatenate([real, imag], -1))
+            got = mm(high, down[0, c]) + mm(low, down[0, c]) + mm(high, down[1, c])
+            if c > 0:
+                got = got + lag[at, :]
+            if c < chunks - 1:
+                lag[at, :] = got
+            else:
+                misfit = got - seen[at, :]
+                weighted = misfit + cubic_weight * misfit * misfit * misfit
+                high, low = split(weighted)
+                whigh[at, :] = high
+                wlow[at, :] = low
+
+        if c == chunks - 2:
+            loads[1].wait()
+    loads[2].wait()
+
+    def swap(c):
+        return remote(
+            sendbuf.at[c, 1 - core, :, real_rows, :], halfbuf.at[c, :, real_rows, :],
+            s1send.at[c], s1recv.at[c], mine, 1 - core,
+        )
+
+    def deliver(c, k):
+        return remote(
+            sumbuf.at[c, other(k), real_rows, :], recvbuf.at[c, k, real_rows, :],
+            s2send.at[c, k], s2recv.at[c, k], other(k), core,
+        )
+
+    def combine(c):
+        swap(c).wait_recv()
+        sumbuf[c] = sendbuf[c, core] + halfbuf[c]
+
+        @pl.loop(1, pairs)
+        def _(k):
+            deliver(c, k).start()
+
+    for c in range(chunks):
+        acc[pl.ds(tile, tile), :] = jnp.zeros((tile, 2 * lanes), f32)
+
+        @pl.loop(0, steps)
+        def _(b):
+            p0 = pl.multiple_of(b * block, block)
+            at = pl.ds(pl.multiple_of(b * span, span), span)
+            high, low = whigh[at, :], wlow[at, :]
+            got = mm(high, up[0, c]) + mm(low, up[0, c]) + mm(high, up[1, c])
+            got = got.reshape(block, tile, 2 * lanes)
+            are, aim = got[:, :, :lanes], got[:, :, lanes:]
+            left = fetched[c, pl.ds(p0, block), :]
+            lre, lim = left[:, None, :lanes], left[:, None, lanes:]
+            right = fetched[c, pl.ds(tile, tile), :]
+            rre, rim = right[None, :, :lanes], right[None, :, lanes:]
+            acc[pl.ds(p0, block), pl.ds(0, lanes)] = jnp.sum(are * rre - aim * rim, 1)
+            acc[pl.ds(p0, block), pl.ds(lanes, lanes)] = jnp.sum(are * rim + aim * rre, 1)
+            acc[pl.ds(tile, tile), pl.ds(0, lanes)] += jnp.sum(are * lre + aim * lim, 0)
+            acc[pl.ds(tile, tile), pl.ds(lanes, lanes)] += jnp.sum(are * lim - aim * lre, 0)
+
+        high, low = split(acc[...])
+        sendbuf[c] = (mm(back, high) + mm(back, low)).reshape(2, pairs, pad, 2 * lanes)
+        swap(c).start()
+        if c > 0:
+            combine(c - 1)
+    combine(chunks - 1)
+
+    for c in range(chunks):
+        @pl.loop(1, pairs)
+        def _(k):
+            deliver(c, k).wait_recv()
+
+        total = sumbuf[c, mine]
+        for k in range(1, pairs):
+            total = total + recvbuf[c, k]
+        total = total * (1.0 / tile)
+        for h in range(2):
+            out_ref[:, h * chunks + c, :] = total[:rows, h * lanes:(h + 1) * lanes]
+
+    for c in range(chunks):
+        forward(c, core).wait_send()
+        swap(c).wait_send()
+
+        @pl.loop(1, pairs)
+        def _(k):
+            spread(c, k, mine).wait_send()
+            deliver(c, k).wait_send()
+
+
+def one_kernel(mesh, spectra, station_place, tiles, observed):
+    n_sta, n_band = mesh.shape["sta"], mesh.shape["band"]
+    n = n_sta * n_band
+    tile, lags = observed.shape[1], observed.shape[3]
+    rows, width = spectra.shape[1], spectra.shape[2]
+    lanes = LANES
+    half = width // 2
+    chunks = half // lanes
+    pad = -(-rows // 8) * 8
+    block = 8
+    down, up = tables(half, lags, lanes)
+    f32, bf16 = jnp.float32, jnp.bfloat16
+    dma = pltpu.SemaphoreType.DMA
+    anywhere = pl.BlockSpec(memory_space=pl.ANY)
+    out = pl.pallas_call(
+        functools.partial(fused, (n_sta, n_band), (tile, rows, pad, lanes, chunks, block)),
+        out_shape=jax.ShapeDtypeStruct((rows, 2 * chunks, lanes), f32),
+        in_specs=[
+            pl.BlockSpec(memory_space=pltpu.SMEM), pl.BlockSpec(memory_space=pltpu.VMEM),
+            anywhere, anywhere, anywhere, anywhere,
+        ],
+        out_specs=pl.BlockSpec(memory_space=pltpu.VMEM),
+        scratch_shapes=[
+            pltpu.VMEM((chunks, 2, n // 2, pad, 2 * lanes), f32),
+            pltpu.VMEM((tile * tile, lags), f32),
+            pltpu.VMEM(down.shape, bf16),
+            pltpu.VMEM(up.shape, bf16),
+            pltpu.VMEM((tile * tile, lags), f32),
+            pltpu.VMEM((tile * tile, lags), bf16),
+            pltpu.VMEM((tile * tile, lags), bf16),
+            pltpu.VMEM((chunks, 2 * tile, 2 * lanes), f32),
+            pltpu.VMEM((2 * tile, 2 * lanes), f32),
+            pltpu.VMEM((chunks, 2, n // 2, pad, 2 * lanes), f32),
+            pltpu.VMEM((chunks, n // 2, pad, 2 * lanes), f32),
+            pltpu.VMEM((chunks, n // 2, pad, 2 * lanes), f32),
+            pltpu.VMEM((chunks, n // 2, pad, 2 * lanes), f32),
+            dma((rows, 2)), dma((3,)),
+            dma((chunks, n // 2)), dma((chunks, n // 2)), dma((chunks,)), dma((chunks,)),
+            dma((chunks,)), dma((chunks,)), dma((chunks, n // 2)), dma((chunks, n // 2)),
+        ],
+        compiler_params=pltpu.CompilerParams(collective_id=0, has_side_effects=True),
+        name="adjoint_kernel",
+    )(
+        tiles, station_place.reshape(1, -1), spectra.reshape(rows, 2 * chunks, lanes),
+        observed.reshape(tile * tile, lags), jnp.asarray(down), jnp.asarray(up),
+    )
+    return out.reshape(1, rows, width)
+
 
 def solution(mesh):
     placed = (
@@ -96,8 +373,17 @@
         P(("grp", "sta", "band"), None),
         P(("grp", "sta", "band"), None, None, None),
     )
+    def body(spectra, station_place, tiles, observed):
+        fits = (
+            mesh.shape["src"] == 1 and mesh.shape["band"] % 2 == 0 and spectra.shape[0] == 1 and tiles.shape[0] == 1
+            and spectra.shape[2] % (2 * LANES) == 0 and observed.shape[1] % 8 == 0
+        )
+        if fits:
+            return one_kernel(mesh, spectra, station_place, tiles, observed)
+        return local(spectra, station_place, tiles, observed)
+
     return jax.shard_map(
-        local,
+        body,
         mesh=mesh,
         in_specs=placed,
         out_specs=P("src", ("grp", "sta", "band"), None),

time: 97 us -> 40 us (0.41); the launches traced: 95.4 us -> 39.8 us
  blocking collectives: 57.2 us -> 0 us
  Pallas kernels: 0 us -> 38.5 us
  matrix products: 16.7 us -> 0 us
  other arithmetic: 9.75 us -> 0 us
  starting transfers between devices: 5.32 us -> 0 us
  local copies, waits for them, and re-layouts: 5.2 us -> 1.35 us
    pallas_call x0 -> x1, Pallas kernels: none -> 38.5 us  [one_kernel(): pl.pallas_call(functools.partial(fused, (n_sta, n_band), (tile, rows, pad...]
    unnamed x1 -> x0, blocking collectives: 32.8 us -> none
    all_gather x1 -> x0, blocking collectives: 24.4 us -> none  [local(): whole = lax.all_gather(spectra[0], ('sta', 'band'), axis=0, tiled=True)]
    dot_general x3 -> x0, matrix products: 16.7 us -> none  [the longest x1 8.3 us: local(): jnp.dot(cross, table, precision=highest, preferred_element_type=jnp.float32)]
    unnamed x4 -> x0, starting transfers between devices: 5.32 us -> none
    dot_general x2 -> x0, other arithmetic: 4.82 us -> none  [the longest x1 3.14 us: adjoint_terms(): jnp.einsum('pqf,sqf->spf', aim, rim, precision=highest)]
    gather x3 -> x0, local copies, waits for them, and re-layouts: 2.05 us -> none  [the longest x2 1.31 us: local(): holder[wanted]]
    cos x1 -> x0, other arithmetic: 1.92 us -> none  [dft_table(): jnp.cos(phase)]
  transfers between devices with their start and end apart: 4 -> 0, of which waited for: 1 -> 0; matrix products, arithmetic and copies ran while one was open for 1% -> 0% of each run, Pallas kernels for 0% -> 0%
where the time goes in v1:
time: 40 us; the launch traced here: 39.8 us
  Pallas kernels  38.5 us (96%)
  local copies, waits for them, and re-layouts  1.35 us (3%)
    pallas_call x1, Pallas kernels, one_kernel(): pl.pallas_call(functools.partial(fused, (n_sta, n_band), (tile, rows, pad...  38.5 us
    unnamed x1, local copies, waits for them, and re-layouts  1.35 us

profile of v1, /device:TPU:0, one launch (start us, length us, event | category | flops | bytes accessed | tf_op | source)
XLA Modules:
  0.0 39.8 jit_solution(9803363250074807308)
XLA Ops:
  0.0 38.5 %adjoint_kernel.1 = f32[6,8,128]{2,1,0:T(8,128)} custom-call(s32[1,2]{1,0:T(1,128)} %pair_ref.1, s32[1,96]{1,0:T(1,128)} %bitcast.7, f32[6,8,128]{2,1,0:T(8,128)} %bitcast.6, f32[2304,256]{1,0:T(8,128)} %bitcast.4, bf16[2,4,256,256]{3,2,1,0:T(8,128)(2,1)} %constant.4.clone.down_hbm, bf16[2,4,256,256]{3,2,1,0:T(8,128)(2,1)} %constant.5.clone.up_hbm), custom_call_target="tpu_custom_call" | custom-call | tf_op jit(solution)/shard_map/adjoint_kernel/pallas_call | solution.py:334
  38.5 1.3 %copy.10 = f32[1,6,1024]{2,0,1:T(1,128)} copy(f32[1,6,1024]{2,0,1:T(1,128)} %bitcast.5) | data formatting | bytes 49152

commit v2 on v1

--- a/solution.py
+++ b/solution.py
@@ -221,7 +221,7 @@
         low = (whole - high.astype(f32) - rest.astype(f32)).astype(jnp.bfloat16)
         fetched[c] = mm(select, high) + mm(select, rest) + mm(select, low)
 
-        @pl.loop(0, steps)
+        @pl.loop(0, steps, unroll=True)
         def _(b):
             p0 = pl.multiple_of(b * block, block)
             at = pl.ds(pl.multiple_of(b * span, span), span)
@@ -271,7 +271,7 @@
     for c in range(chunks):
         acc[pl.ds(tile, tile), :] = jnp.zeros((tile, 2 * lanes), f32)
 
-        @pl.loop(0, steps)
+        @pl.loop(0, steps, unroll=True)
         def _(b):
             p0 = pl.multiple_of(b * block, block)
             at = pl.ds(pl.multiple_of(b * span, span), span)

time: 40 us -> 33.9 us (0.85)
  Pallas kernels: 38.5 us -> 32.3 us
    pallas_call x1, Pallas kernels: 38.5 us -> 32.3 us  [one_kernel(): pl.pallas_call(functools.partial(fused, (n_sta, n_band), (tile, rows, pad...]
where the time goes in v2:
time: 33.9 us; the launch traced here: 33.7 us
  Pallas kernels  32.3 us (95%)
  local copies, waits for them, and re-layouts  1.35 us (4%)
    pallas_call x1, Pallas kernels, one_kernel(): pl.pallas_call(functools.partial(fused, (n_sta, n_band), (tile, rows, pad...  32.3 us
    unnamed x1, local copies, waits for them, and re-layouts  1.35 us

profile of v2, /device:TPU:0, one launch (start us, length us, event | category | flops | bytes accessed | tf_op | source)
XLA Modules:
  0.0 33.7 jit_solution(15216870990451046758)
XLA Ops:
  0.0 32.3 %adjoint_kernel.1 = f32[6,8,128]{2,1,0:T(8,128)} custom-call(s32[1,2]{1,0:T(1,128)} %pair_ref.1, s32[1,96]{1,0:T(1,128)} %bitcast.7, f32[6,8,128]{2,1,0:T(8,128)} %bitcast.6, f32[2304,256]{1,0:T(8,128)} %bitcast.4, bf16[2,4,256,256]{3,2,1,0:T(8,128)(2,1)} %constant.4.clone.down_hbm, bf16[2,4,256,256]{3,2,1,0:T(8,128)(2,1)} %constant.5.clone.up_hbm), custom_call_target="tpu_custom_call" | custom-call | tf_op jit(solution)/shard_map/adjoint_kernel/pallas_call | solution.py:334
  32.4 1.3 %copy.10 = f32[1,6,1024]{2,0,1:T(1,128)} copy(f32[1,6,1024]{2,0,1:T(1,128)} %bitcast.5) | data formatting | bytes 49152
